TPU v7x, 32 devices: a whole 2x2x4 slice. The times are simulated.
32 devices in a mesh: row: 4 (over x, core), col: 8 (over z, y).
Axes of the slice: x: 2, y: 2, z: 4, core: 2. Of those that a mesh axis runs over, the one named last changes fastest.
Arguments:
- front_panels: float32 [16, 4, 256, 8, 8, 256], P(None, 'row', 'col'), as said below
- child_update_tiles: float32 [4, 8, 8, 256, 256], P('row', 'col'), may hold values from -2 to 2
- child_rows: int32 [4, 8, 8], P('row', 'col'), may hold values from 0 to 63, as said below
- child_cols: int32 [4, 8, 8], P('row', 'col'), may hold values from 0 to 7
- child_counts: int32 [4, 8], P('row', 'col'), may hold values from 4 to 8, as said below
- row_maps: int32 [4, 8, 8, 256], P('row', 'col'), may hold values from 0 to 255, each once within a row
- col_maps: int32 [4, 8, 8, 256], P('row', 'col'), may hold values from 0 to 255, each once within a row
Outputs:
- factored_front: float32 [16, 4, 256, 8, 8, 256], P(None, 'row', None, None, 'col')
Inputs may be any that keep to these rules, and one draw needn't show every extreme that they name: child_rows[r, c, k] modulo 4 names one of four owner rows; among the live slots of one device at most 2 name the same owner row, and some device sends exactly 2 to some owner; every slot's target tile column is at most its target tile row. `child_counts`: every device of col index 0 has all slots live. `front_panels`: the diagonal of the front dominates its first tile, so that tile stays positive definite after the children are added.
All inputs are finite; a program needn't handle non-finite values.
Results may differ from a plain program's by a relative error of at most 0.0003.
Values sent between devices are 32-bit elements; how exact they have to be, the bound alone decides.
No kernel may reach another device: no remote copies, remote signals or barrier semaphores. Data moves between devices by JAX's collectives and lax.ppermute only.
A program may use at most 320 MiB of HBM per device.

v0:
```python
import jax
import jax.numpy as jnp
from jax import lax
from jax.sharding import PartitionSpec as P


def broadcast(value, axis, source):
    kept = jnp.where(lax.axis_index(axis) == source, value, 0).astype(value.dtype)
    return lax.psum(kept, axis)


def slot_positions(owners, is_live):
    slot_entries = owners.shape[-1]
    earlier = lax.broadcasted_iota(
        jnp.int32, (slot_entries, slot_entries), 0
    ) < lax.broadcasted_iota(jnp.int32, (slot_entries, slot_entries), 1)
    same_owner = (owners[..., :, None] == owners[..., None, :]) & is_live[..., :, None] & earlier
    return jnp.sum(same_owner.astype(jnp.int32), axis=-2)


def on_device(
    front_panels, child_update_tiles, child_rows, child_cols, child_counts, row_maps, col_maps
):
    largest_index = lax.Precision.HIGHEST
    row_size = lax.axis_size("row")
    col_size = lax.axis_size("col")
    my_row = lax.axis_index("row")
    my_col = lax.axis_index("col")
    front_width = front_panels.shape[-1]
    blocks = lax.all_to_all(front_panels, "col", split_axis=4, concat_axis=2, tiled=True)
    row_tiles = blocks.shape[0]
    col_tiles = blocks.shape[3]
    blocks = blocks.reshape(row_tiles, front_width, col_tiles, front_width)
    slot_entries = child_update_tiles.shape[2]
    capacity = slot_entries // 4
    labels = lax.broadcasted_iota(jnp.int32, (1, 1, front_width), 2)
    row_indicator = (row_maps.reshape(slot_entries, front_width)[:, :, None] == labels).astype(
        jnp.float32
    )
    column_indicator = (col_maps.reshape(slot_entries, front_width)[:, :, None] == labels).astype(
        jnp.float32
    )
    shifted_tiles = jnp.einsum(
        "gml,gmq->glq",
        row_indicator,
        child_update_tiles.reshape(slot_entries, front_width, front_width),
        precision=largest_index,
    )
    shifted_tiles = jnp.einsum(
        "afb,abx->afx", shifted_tiles, column_indicator, precision=largest_index
    )
    slot_ids = lax.broadcasted_iota(jnp.int32, (slot_entries,), 0)
    is_live = slot_ids < child_counts.reshape(())
    owners = child_rows.reshape(slot_entries) % row_size
    positions = slot_positions(owners, is_live)
    dest_ids = lax.broadcasted_iota(jnp.int32, (row_size, capacity, slot_entries), 0)
    place_ids = lax.broadcasted_iota(jnp.int32, (row_size, capacity, slot_entries), 1)
    selector = (
        (owners[None, None, :] == dest_ids)
        & (positions[None, None, :] == place_ids)
        & is_live[None, None, :]
    ).astype(jnp.float32)
    outgoing = jnp.einsum(
        "opk,kx->opx",
        selector,
        shifted_tiles.reshape(slot_entries, front_width * front_width),
        precision=largest_index,
    )
    incoming = lax.all_to_all(outgoing, "row", split_axis=0, concat_axis=0, tiled=True)
    all_rows, all_cols, all_counts = (
        lax.all_gather(child_rows, "row", axis=0, tiled=True),
        lax.all_gather(child_cols, "row", axis=0, tiled=True),
        lax.all_gather(child_counts, "row", axis=0, tiled=True),
    )
    source_rows = all_rows.reshape(row_size, slot_entries)
    source_cols = all_cols.reshape(row_size, slot_entries)
    source_live = slot_ids[None, :] < all_counts.reshape(row_size)[:, None]
    source_owner = source_rows % row_size
    source_pos = slot_positions(source_owner, source_live)
    mine = (source_live & (source_owner == my_row)).astype(jnp.float32)
    depth_onehot = (
        (source_rows // row_size)[:, :, None]
        == lax.broadcasted_iota(jnp.int32, (1, 1, row_tiles), 2)
    ).astype(jnp.float32) * mine[:, :, None]
    across_onehot = (
        source_cols[:, :, None] == lax.broadcasted_iota(jnp.int32, (1, 1, col_tiles), 2)
    ).astype(jnp.float32)
    place_onehot = (
        source_pos[:, :, None] == lax.broadcasted_iota(jnp.int32, (1, 1, capacity), 2)
    ).astype(jnp.float32)
    landing = jnp.einsum(
        "ska,skb,skp->absp", depth_onehot, across_onehot, place_onehot, precision=largest_index
    )
    incoming = incoming.reshape(row_size, capacity, front_width, front_width)
    blocks = blocks + jnp.einsum("absp,spxy->axby", landing, incoming, precision=largest_index)
    tile_i = lax.broadcasted_iota(jnp.int32, (row_tiles, 1, col_tiles, 1), 0) * row_size + my_row
    tile_j = lax.broadcasted_iota(jnp.int32, (row_tiles, 1, col_tiles, 1), 2) * col_size + my_col
    flipped = jnp.einsum("axby->aybx", blocks)
    blocks = jnp.where(tile_i == tile_j, 0.5 * (blocks + flipped), blocks)
    identity = jnp.eye(front_width, dtype=jnp.float32)
    corner = blocks[0, :, 0, :]
    at_root = (my_row == 0) & (my_col == 0)
    factor = jnp.linalg.cholesky(jnp.where(at_root, corner, identity))
    factor = broadcast(factor, "row", 0)
    column = blocks[:, :, 0, :].reshape(row_tiles * front_width, front_width)
    solved = jax.scipy.linalg.solve_triangular(factor, column.T, lower=True).T.reshape(
        row_tiles, front_width, front_width
    )
    tile_index = lax.broadcasted_iota(jnp.int32, (row_tiles, 1, 1), 0) * row_size + my_row
    kept = jnp.where(tile_index == 0, factor[None, :, :], solved)
    below = jnp.where(tile_index == 0, 0.0, solved)
    row_panel = broadcast(below, "col", 0)
    group = col_size // row_size
    whole = lax.all_gather(row_panel, "row", axis=0, tiled=True)
    whole = whole.reshape(row_size, col_tiles, group, front_width, front_width)
    picked = lax.dynamic_index_in_dim(whole, my_col % row_size, 0, keepdims=False)
    col_panel = lax.dynamic_index_in_dim(picked, my_col // row_size, 1, keepdims=False)
    blocks = blocks - jnp.einsum("asx,bqx->asbq", row_panel, col_panel, precision=largest_index)
    first_column = jnp.where(my_col == 0, kept, blocks[:, :, 0, :])
    blocks = blocks.at[:, :, 0, :].set(first_column)
    blocks = jnp.where(tile_i >= tile_j, blocks, 0.0)
    return blocks.reshape(row_tiles, 1, front_width, col_tiles, 1, front_width)


def solution(mesh):
    return jax.shard_map(
        on_device,
        mesh=mesh,
        in_specs=(
            P(None, "row", "col", None, None, None),
            P("row", "col", None, None, None),
            P("row", "col", None),
            P("row", "col", None),
            P("row", "col"),
            P("row", "col", None, None),
            P("row", "col", None, None),
        ),
        out_specs=P(None, "row", None, None, "col", None),
        check_vma=False,
    )
```

profile of v0, /device:TPU:0, one launch (start us, length us, event | category | flops | bytes accessed | tf_op | source)
XLA Modules:
  0.0 1470.2 jit_solution(9605571834959242759)
XLA Ops:
  15.7 4.1 fusion.33
  19.8 4.2 all-to-all-start.1
  24.0 30.6 %copy.67 = f32[16,1,32,8,8,256]{5,3,2,0,1,4:T(8,128)} copy(f32[16,1,32,8,8,256]{5,4,3,2,1,0:T(8,128)} %param.9) | data formatting | bytes 67108864 | tf_op args[0]
  55.9 7.1 all-to-all-start
  64.2 5.8 all-reduce.1
  70.0 5.0 all_gather.14
  75.0 5.2 all_gather.17
  84.8 30.9 %convolution_bitcast_fusion = f32[256,256,16,8]{1,2,3,0:T(8,128)} fusion(f32[4,2,256,256,1]{3,2,1,0,4:T(8,128)S(1)} %bitcast.110, f32[16,8,4,2]{0,1,3,2:T(8,128)S(1)} %convolution_bitcast_fusion.1), kind=kOutput, calls=%fused_computation.8 | convolution fusion | flops 805306368 | bytes 35655680 | tf_op jit(solution)/shard_map/absp,spxy->axby/dot_general | solution.py:95
  115.7 34.4 %copy.72 = f32[256,256,16,8]{0,1,3,2:T(8,128)} copy(f32[256,256,16,8]{1,2,3,0:T(8,128)} %convolution_bitcast_fusion) | data formatting | bytes 67108864 | tf_op jit(solution)/shard_map/absp,spxy->axby/dot_general | solution.py:95
  150.2 637.7 %all-to-all-done = f32[16,1,32,8,8,256]{5,3,2,0,1,4:T(8,128)} async-done(((f32[16,1,32,8,8,256]{5,3,2,0,1,4:T(8,128)}), f32[16,1,32,8,8,256]{5,3,2,0,1,4:T(8,128)}, u32[]{:S(2)}, u32[]{:S(2)}) %all-to-all-start) | async-done | bytes 33554464 | tf_op jit(solution)/shard_map/all_to_all | solution.py:30
  787.9 22.9 %copy.68 = f32[16,1,32,8,8,256]{5,3,2,4,0,1:T(8,128)} copy(f32[16,1,32,8,8,256]{5,3,2,0,1,4:T(8,128)} %all-to-all-done) | data formatting | bytes 67108864 | tf_op jit(solution)/shard_map/all_to_all | solution.py:30
  810.7 35.0 %copy.73 = f32[16,256,8,256]{1,3,2,0:T(8,128)} copy(f32[16,256,8,256]{3,2,1,0:T(8,128)} %bitcast.104) | data formatting | bytes 67108864 | tf_op jit(solution)/shard_map/reshape | solution.py:33
  845.7 33.5 %bitcast_add_fusion.1 = f32[16,256,8,256]{1,3,2,0:T(8,128)} fusion(f32[16,256,8,256]{1,3,2,0:T(8,128)} %copy.73, f32[256,256,16,8]{0,1,3,2:T(8,128)} %copy.72), kind=kLoop, calls=%fused_computation.5 | loop fusion | flops 8388608 | bytes 100663296 | tf_op jit(solution)/shard_map/add | solution.py:95
  879.2 31.9 %copy.74 = f32[16,256,8,256]{3,1,2,0:T(8,128)} copy(f32[16,256,8,256]{1,3,2,0:T(8,128)} %bitcast_add_fusion.1) | data formatting | bytes 67108864 | tf_op jit(solution)/shard_map/add | solution.py:95
  911.2 33.6 %fusion.1 = f32[16,256,8,256]{1,3,2,0:T(8,128)} fusion(f32[16,256,8,256]{1,3,2,0:T(8,128)} %bitcast_add_fusion.1, f32[16,256,8,256]{3,1,2,0:T(8,128)} %copy.74, pred[16,8]{1,0:T(8,128)(4,1)S(1)} %get-tuple-element.42), kind=kLoop, calls=%fused_computation.4 | loop fusion | flops 25165824 | bytes 100663424 | tf_op jit(solution)/shard_map/jit(_where)/select_n | solution.py:99
  947.0 11.7 cholesky.50
  958.7 9.8 custom-call.15
  969.0 11.7 cholesky.105
  983.6 4.5 slice.96
  988.1 5.8 copy.76
  993.9 5.7 copy.77
  999.6 14.6 all-reduce.5.cloned.1.call-done
  1019.0 19.7 %custom-call.16 = f32[2,128,128]{1,2,0:T(8,128)S(1)} custom-call(f32[2,128,128]{2,1,0:T(8,128)S(1)} %get-tuple-element.24), custom_call_target="InvertDiagBlocksLowerTriangular" | custom-call | tf_op jit(solution)/shard_map/jit(_solve_triangular)/triangular_solve | solution.py:106
  1048.6 5.6 copy.94
  1054.2 4.7 select_select_fusion
  1059.0 156.4 %all-reduce.7.cloned.1.call-done = f32[16,256,256]{2,1,0:T(8,128)} async-done(((f32[16,256,256]{2,1,0:T(8,128)}), f32[16,256,256]{2,1,0:T(8,128)}) %all-reduce.7.cloned.1.call-update) | async-done | bytes 4194320 | tf_op jit(solution)/shard_map/psum | solution.py:9
  1215.5 5.6 copy.83
  1221.2 100.9 %all-gather.2.cloned.1.call-done = f32[64,256,256]{2,1,0:T(8,128)} async-done(((f32[16,256,256]{2,1,0:T(8,128)}), f32[64,256,256]{2,1,0:T(8,128)}) %all-gather.2.cloned.1.call-update) | async-done | bytes 16777232 | tf_op jit(solution)/shard_map/all_gather | solution.py:114
  1322.0 35.3 %convolution_subtract_fusion = f32[16,256,8,256]{1,3,2,0:T(8,128)} fusion(f32[16,256,8,256]{1,3,2,0:T(8,128)} %fusion.1, f32[16,256,256]{2,1,0:T(8,128)} %all-reduce.7.cloned.1.call-done, f32[4,8,2,256,256]{4,3,2,1,0:T(8,128)} %bitcast.111, s32[]{:T(128)S(6)} %select_n.139, s32[]{:T(128)S(6)} %select_n.142), kind=kOutput, calls=%fused_computation.7 | convolution fusion | flops 25778192384 | bytes 73400328 | tf_op jit(solution)/shard_map/asx,bqx->asbq/dot_general | solution.py:118
  1357.3 4.8 fusion.2
  1362.2 22.9 %select_bitcast_fusion = f32[16,1,256,8,1,256]{2,5,3,0,4,1:T(8,128)} fusion(f32[16,256,8,256]{1,3,2,0:T(8,128)} %fusion.2, pred[16,8]{1,0:T(8,128)(4,1)S(1)} %copy-done.6), kind=kLoop, calls=%fused_computation.6 | loop fusion | flops 8388608 | bytes 67108992 | tf_op jit(solution)/shard_map/reshape | solution.py:122
  1385.1 78.3 %copy.84 = f32[16,1,256,8,1,256]{5,4,3,2,1,0:T(1,128)} copy(f32[16,1,256,8,1,256]{2,5,3,0,4,1:T(8,128)} %select_bitcast_fusion) | data formatting | bytes 67108864 | tf_op jit(solution)/shard_map/reshape | solution.py:122
  (80 shorter events, 38.6 us)
Async XLA Ops:
  6.5 1.6 copy-start
  6.5 3.8 copy-start.7
  19.8 34.8 %all-to-all-start.1 = ((f32[4,2,65536]{2,1,0:T(2,128)}), f32[4,2,65536]{2,1,0:T(2,128)S(1)}, u32[]{:S(2)}, u32[]{:S(2)}) async-start(f32[4,2,65536]{2,1,0:T(2,128)} %fusion.33), calls=%async_computation.1 | async-start | bytes 4194304 | tf_op jit(solution)/shard_map/all_to_all | solution.py:69
  54.6 8.5 copy-start.10
  54.6 15.4 %copy-start.8 = (s32[1,1,8]{2,1,0:T(1,128)S(1)}, s32[1,1,8]{2,1,0:T(1,128)}, u32[]{:S(2)}) copy-start(s32[1,1,8]{2,1,0:T(1,128)} %param.11) | copy-start | bytes 100
  54.6 20.5 %copy-start.9 = (s32[1,1,8]{2,1,0:T(1,128)S(1)}, s32[1,1,8]{2,1,0:T(1,128)}, u32[]{:S(2)}) copy-start(s32[1,1,8]{2,1,0:T(1,128)} %param.12) | copy-start | bytes 100
  54.6 1.3 copy-start.4
  55.9 731.9 %all-to-all-start = ((f32[16,1,32,8,8,256]{5,3,2,0,1,4:T(8,128)}), f32[16,1,32,8,8,256]{5,3,2,0,1,4:T(8,128)}, u32[]{:S(2)}, u32[]{:S(2)}) async-start(f32[16,1,32,8,8,256]{5,3,2,0,1,4:T(8,128)} %copy.67), calls=%async_computation | async-start | bytes 67108864 | tf_op jit(solution)/shard_map/all_to_all | solution.py:30
  63.0 951.1 %all-reduce.5.cloned.1.call-start = ((), (), s32[]{:S(2)}) async-start(), calls=%async_computation.2 | async-start | bytes 524288 | tf_op jit(solution)/shard_map/psum | solution.py:9
  983.5 231.9 %all-reduce.7.cloned.1.call-start = ((), (), s32[]{:S(2)}) async-start(), calls=%async_computation.3 | async-start | bytes 8388608 | tf_op jit(solution)/shard_map/psum | solution.py:9
  1038.7 3.7 copy-start.3
  1059.0 263.1 %all-gather.2.cloned.1.call-start = ((), (), s32[]{:S(2)}) async-start(), calls=%async_computation.4 | async-start | bytes 20971520 | tf_op jit(solution)/shard_map/all_gather | solution.py:114
  1215.5 5.6 copy-start.5
  1322.0 35.3 %copy-start.2 = (f32[16,256,1,256]{1,3,2,0:T(8,128)S(1)}, f32[16,256,1,256]{1,3,2,0:T(8,128)}, u32[]{:S(2)}) copy-start(f32[16,256,1,256]{1,3,2,0:T(8,128)} %copy.83) | copy-start | bytes 12582916
  1357.3 4.8 copy-start.6
  1385.1 78.3 %copy-start.1 = (f32[1,1,8,256,256]{4,3,2,1,0:T(8,128)S(1)}, f32[1,1,8,256,256]{4,3,2,1,0:T(8,128)}, u32[]{:S(2)}) copy-start(f32[1,1,8,256,256]{4,3,2,1,0:T(8,128)} %param.10) | copy-start | bytes 6291460
Sparse Core Ops, SparseCore 0:
  983.6 30.4 all-reduce.4
  1059.1 156.2 all-reduce.6
  1217.1 104.9 all-gather.1
where the time goes:
time: 1480 us; the launch traced here: 1470 us
  waiting for transfers between devices  910 us (61%)
  local copies, waits for them, and re-layouts  273 us (18%)
  other arithmetic  162 us (11%)
  matrix products  83.3 us (6%)
  blocking collectives  16 us (1%)
  between operations  15.5 us (1%)
    all_to_all x1, waiting for transfers between devices, on_device(): lax.all_to_all(front_panels, 'col', split_axis=4, concat_axis=2, tiled=True)  638 us
    psum x2, waiting for transfers between devices, broadcast(): return lax.psum(kept, axis)  171 us
    all_gather x1, waiting for transfers between devices, on_device(): whole = lax.all_gather(row_panel, 'row', axis=0, tiled=True)  101 us
    reshape x1, local copies, waits for them, and re-layouts, on_device(): return blocks.reshape(row_tiles, 1, front_width, col_tiles, 1, front_width)  78.3 us
    dot_general x1, matrix products, on_device(): jnp.einsum('asx,bqx->asbq', row_panel, col_panel, precision=largest_index)  35.3 us
    reshape x1, local copies, waits for them, and re-layouts, on_device(): blocks = blocks.reshape(row_tiles, front_width, col_tiles, front_width)  35 us
    dot_general x1, local copies, waits for them, and re-layouts, on_device(): jnp.einsum('absp,spxy->axby', landing, incoming, precision=largest_index)  34.4 us
    another operation x6, other arithmetic, on_device(): factor = jnp.linalg.cholesky(jnp.where(at_root, corner, identity))  34 us
  transfers between devices with their start and end apart: 5, of which 4 were waited for; matrix products, arithmetic and copies ran while one was open for 8% of the time, Pallas kernels for 0%

commit v1 on v0

--- a/solution.py
+++ b/solution.py
@@ -27,7 +27,12 @@
     my_row = lax.axis_index("row")
     my_col = lax.axis_index("col")
     front_width = front_panels.shape[-1]
-    blocks = lax.all_to_all(front_panels, "col", split_axis=4, concat_axis=2, tiled=True)
+    blocks = jnp.concatenate(
+        lax.all_to_all(
+            jnp.stack(jnp.split(front_panels, lax.axis_size("col"), axis=4)), "col", 0, 0
+        ),
+        axis=2,
+    )
     row_tiles = blocks.shape[0]
     col_tiles = blocks.shape[3]
     blocks = blocks.reshape(row_tiles, front_width, col_tiles, front_width)

time: 1480 us -> 1570 us (1.061)
  local copies, waits for them, and re-layouts: 273 us -> 364 us
    split x0 -> x1, local copies, waits for them, and re-layouts: none -> 92.8 us  [on_device(): jnp.split(front_panels, lax.axis_size('col'), axis=4)]
    another operation x6 -> x8, local copies, waits for them, and re-layouts: 3.82 us -> 41 us  [the longest x1 35 us: on_device(): blocks = blocks.reshape(row_tiles, front_width, col_tiles, front_width)]
    reshape x1 -> x0, local copies, waits for them, and re-layouts: 35 us -> none  [on_device(): blocks = blocks.reshape(row_tiles, front_width, col_tiles, front_width)]
    unnamed x26 -> x46, local copies, waits for them, and re-layouts: 33.2 us -> 29.6 us
  transfers between devices with their start and end apart: 5 -> 5, of which waited for: 4 -> 4; matrix products, arithmetic and copies ran while one was open for 8% -> 13% of each run, Pallas kernels for 0% -> 0%
where the time goes in v1:
time: 1570 us; the launch traced here: 1560 us
  waiting for transfers between devices  910 us (58%)
  local copies, waits for them, and re-layouts  364 us (23%)
  other arithmetic  162 us (10%)
  matrix products  83.3 us (5%)
  blocking collectives  15.8 us (1%)
    all_to_all x1, waiting for transfers between devices, on_device(): lax.all_to_all(jnp.stack(jnp.split(front_panels, lax.axis_size('col'), ax...  638 us
    psum x2, waiting for transfers between devices, broadcast(): return lax.psum(kept, axis)  171 us
    all_gather x1, waiting for transfers between devices, on_device(): whole = lax.all_gather(row_panel, 'row', axis=0, tiled=True)  101 us
    split x1, local copies, waits for them, and re-layouts, on_device(): jnp.split(front_panels, lax.axis_size('col'), axis=4)  92.8 us
    reshape x1, local copies, waits for them, and re-layouts, on_device(): return blocks.reshape(row_tiles, 1, front_width, col_tiles, 1, front_width)  78.3 us
    dot_general x1, matrix products, on_device(): jnp.einsum('asx,bqx->asbq', row_panel, col_panel, precision=largest_index)  35.3 us
    another operation x1, local copies, waits for them, and re-layouts, on_device(): blocks = blocks.reshape(row_tiles, front_width, col_tiles, front_width)  35 us
    dot_general x1, local copies, waits for them, and re-layouts, on_device(): jnp.einsum('absp,spxy->axby', landing, incoming, precision=largest_index)  34.4 us
  transfers between devices with their start and end apart: 5, of which 4 were waited for; matrix products, arithmetic and copies ran while one was open for 13% of the time, Pallas kernels for 0%

profile of v1, /device:TPU:0, one launch (start us, length us, event | category | flops | bytes accessed | tf_op | source)
XLA Modules:
  0.0 1561.6 jit_solution(3904566239132187786)
XLA Ops:
  19.6 4.2 all-to-all-start.1
  23.8 92.8 %fusion.53 = (f32[16,1,32,8,1,256]{5,4,3,2,1,0:T(1,128)}, f32[16,1,32,8,1,256]{5,4,3,2,1,0:T(1,128)}, f32[16,1,32,8,1,256]{5,4,3,2,1,0:T(1,128)}, f32[16,1,32,8,...) fusion(f32[16,1,32,8,8,256]{5,4,3,2,1,0:T(8,128)} %param.9), kind=kLoop, calls=%fused_computation.126 | loop fusion | bytes 67108864 | tf_op jit(solution)/shard_map/split | solution.py:32
  116.6 4.7 fusion.10
  147.4 7.3 all-to-all-start
  156.0 5.8 all-reduce.1
  161.8 5.0 all_gather.14
  166.8 5.0 all_gather.17
  176.4 30.9 %convolution_bitcast_fusion = f32[256,256,16,8]{1,2,3,0:T(8,128)} fusion(f32[4,2,256,256,1]{3,2,1,0,4:T(8,128)S(1)} %bitcast.140, f32[16,8,4,2]{0,1,3,2:T(8,128)S(1)} %convolution_bitcast_fusion.1), kind=kOutput, calls=%fused_computation.8 | convolution fusion | flops 805306368 | bytes 35655680 | tf_op jit(solution)/shard_map/absp,spxy->axby/dot_general | solution.py:100
  207.3 34.4 %copy.100 = f32[256,256,16,8]{0,1,3,2:T(8,128)} copy(f32[256,256,16,8]{1,2,3,0:T(8,128)} %convolution_bitcast_fusion) | data formatting | bytes 67108864 | tf_op jit(solution)/shard_map/absp,spxy->axby/dot_general | solution.py:100
  241.7 637.7 %all-to-all-done = f32[8,16,1,32,8,1,256]{6,4,3,1,5,2,0:T(8,128)} async-done(((f32[8,16,1,32,8,1,256]{6,4,3,1,5,2,0:T(8,128)}), f32[8,16,1,32,8,1,256]{6,4,3,1,5,2,0:T(8,128)}, u32[]{:S(2)}, u32[]{:S(2)}) %all-to-all-start) | async-done | bytes 33554464 | tf_op jit(solution)/shard_map/all_to_all | solution.py:31
  879.5 22.9 %copy.96 = f32[8,16,1,32,8,1,256]{6,4,3,0,1,5,2:T(8,128)} copy(f32[8,16,1,32,8,1,256]{6,4,3,1,5,2,0:T(8,128)} %all-to-all-done) | data formatting | bytes 67108864 | tf_op jit(solution)/shard_map/all_to_all | solution.py:31
  902.3 35.0 %copy.101 = f32[16,256,8,256]{1,3,2,0:T(8,128)} copy(f32[16,256,8,256]{3,2,1,0:T(8,128)} %bitcast.134) | data formatting | bytes 67108864 | tf_op jit(solution)/shard_map/reshape;reshape | solution.py:38
  937.3 33.5 %bitcast_add_fusion.1 = f32[16,256,8,256]{1,3,2,0:T(8,128)} fusion(f32[16,256,8,256]{1,3,2,0:T(8,128)} %copy.101, f32[256,256,16,8]{0,1,3,2:T(8,128)} %copy.100), kind=kLoop, calls=%fused_computation.5 | loop fusion | flops 8388608 | bytes 100663296 | tf_op jit(solution)/shard_map/add | solution.py:100
  970.9 32.0 %copy.102 = f32[16,256,8,256]{3,1,2,0:T(8,128)} copy(f32[16,256,8,256]{1,3,2,0:T(8,128)} %bitcast_add_fusion.1) | data formatting | bytes 67108864 | tf_op jit(solution)/shard_map/add | solution.py:100
  1002.9 33.6 %fusion.1 = f32[16,256,8,256]{1,3,2,0:T(8,128)} fusion(f32[16,256,8,256]{1,3,2,0:T(8,128)} %bitcast_add_fusion.1, f32[16,256,8,256]{3,1,2,0:T(8,128)} %copy.102, pred[16,8]{1,0:T(8,128)(4,1)S(1)} %get-tuple-element.50), kind=kLoop, calls=%fused_computation.4 | loop fusion | flops 25165824 | bytes 100663424 | tf_op jit(solution)/shard_map/jit(_where)/select_n | solution.py:104
  1038.6 11.7 cholesky.50
  1050.4 9.8 custom-call.15
  1060.7 11.7 cholesky.105
  1075.3 4.5 slice.96
  1079.8 5.8 copy.104
  1085.6 5.7 copy.105
  1091.3 14.5 all-reduce.5.cloned.1.call-done
  1110.4 19.7 %custom-call.16 = f32[2,128,128]{1,2,0:T(8,128)S(1)} custom-call(f32[2,128,128]{2,1,0:T(8,128)S(1)} %get-tuple-element.24), custom_call_target="InvertDiagBlocksLowerTriangular" | custom-call | tf_op jit(solution)/shard_map/jit(_solve_triangular)/triangular_solve | solution.py:111
  1140.0 5.6 copy.122
  1145.7 4.7 select_select_fusion
  1150.4 156.4 %all-reduce.7.cloned.1.call-done = f32[16,256,256]{2,1,0:T(8,128)} async-done(((f32[16,256,256]{2,1,0:T(8,128)}), f32[16,256,256]{2,1,0:T(8,128)}) %all-reduce.7.cloned.1.call-update) | async-done | bytes 4194320 | tf_op jit(solution)/shard_map/psum | solution.py:9
  1306.9 5.6 copy.111
  1312.6 100.9 %all-gather.2.cloned.1.call-done = f32[64,256,256]{2,1,0:T(8,128)} async-done(((f32[16,256,256]{2,1,0:T(8,128)}), f32[64,256,256]{2,1,0:T(8,128)}) %all-gather.2.cloned.1.call-update) | async-done | bytes 16777232 | tf_op jit(solution)/shard_map/all_gather | solution.py:119
  1413.5 35.3 %convolution_subtract_fusion = f32[16,256,8,256]{1,3,2,0:T(8,128)} fusion(f32[16,256,8,256]{1,3,2,0:T(8,128)} %fusion.1, f32[16,256,256]{2,1,0:T(8,128)} %all-reduce.7.cloned.1.call-done, f32[4,8,2,256,256]{4,3,2,1,0:T(8,128)} %bitcast.141, s32[]{:T(128)S(6)} %select_n.139, s32[]{:T(128)S(6)} %select_n.142), kind=kOutput, calls=%fused_computation.7 | convolution fusion | flops 25778192384 | bytes 73400328 | tf_op jit(solution)/shard_map/asx,bqx->asbq/dot_general | solution.py:123
  1448.8 4.8 fusion.2
  1453.6 22.9 %select_bitcast_fusion = f32[16,1,256,8,1,256]{2,5,3,0,4,1:T(8,128)} fusion(f32[16,256,8,256]{1,3,2,0:T(8,128)} %fusion.2, pred[16,8]{1,0:T(8,128)(4,1)S(1)} %copy-done.13), kind=kLoop, calls=%fused_computation.6 | loop fusion | flops 8388608 | bytes 67108992 | tf_op jit(solution)/shard_map/reshape | solution.py:127
  1476.5 78.3 %copy.112 = f32[16,1,256,8,1,256]{5,4,3,2,1,0:T(1,128)} copy(f32[16,1,256,8,1,256]{2,5,3,0,4,1:T(8,128)} %select_bitcast_fusion) | data formatting | bytes 67108864 | tf_op jit(solution)/shard_map/reshape | solution.py:127
  (102 shorter events, 66.7 us)
Async XLA Ops:
  6.5 2.1 copy-start
  6.5 4.4 copy-start.14
  19.6 126.4 %all-to-all-start.1 = ((f32[4,2,65536]{2,1,0:T(2,128)}), f32[4,2,65536]{2,1,0:T(2,128)S(1)}, u32[]{:S(2)}, u32[]{:S(2)}) async-start(f32[4,2,65536]{2,1,0:T(2,128)} %fusion.41), calls=%async_computation.1 | async-start | bytes 4194304 | tf_op jit(solution)/shard_map/all_to_all | solution.py:74
  116.6 4.7 copy-start.9
  121.4 3.7 copy-start.8
  125.1 3.7 copy-start.7
  128.8 3.7 copy-start.5
  132.5 3.7 copy-start.4
  136.2 3.7 copy-start.3
  139.9 3.7 copy-start.2
  146.0 8.7 copy-start.17
  146.0 15.7 %copy-start.15 = (s32[1,1,8]{2,1,0:T(1,128)S(1)}, s32[1,1,8]{2,1,0:T(1,128)}, u32[]{:S(2)}) copy-start(s32[1,1,8]{2,1,0:T(1,128)} %param.11) | copy-start | bytes 100
  146.0 20.8 %copy-start.16 = (s32[1,1,8]{2,1,0:T(1,128)S(1)}, s32[1,1,8]{2,1,0:T(1,128)}, u32[]{:S(2)}) copy-start(s32[1,1,8]{2,1,0:T(1,128)} %param.12) | copy-start | bytes 100
  146.0 1.3 copy-start.11
  147.4 732.1 %all-to-all-start = ((f32[8,16,1,32,8,1,256]{6,4,3,1,5,2,0:T(8,128)}), f32[8,16,1,32,8,1,256]{6,4,3,1,5,2,0:T(8,128)}, u32[]{:S(2)}, u32[]{:S(2)}) async-start(f32[8,16,1,32,8,1,256]{6,4,3,1,5,2,0:T(8,128)} %fusion.3), calls=%async_computation | async-start | bytes 67108864 | tf_op jit(solution)/shard_map/all_to_all | solution.py:31
  154.6 951.2 %all-reduce.5.cloned.1.call-start = ((), (), s32[]{:S(2)}) async-start(), calls=%async_computation.2 | async-start | bytes 524288 | tf_op jit(solution)/shard_map/psum | solution.py:9
  1075.2 231.7 %all-reduce.7.cloned.1.call-start = ((), (), s32[]{:S(2)}) async-start(), calls=%async_computation.3 | async-start | bytes 8388608 | tf_op jit(solution)/shard_map/psum | solution.py:9
  1130.1 3.7 copy-start.10
  1150.4 263.1 %all-gather.2.cloned.1.call-start = ((), (), s32[]{:S(2)}) async-start(), calls=%async_computation.4 | async-start | bytes 20971520 | tf_op jit(solution)/shard_map/all_gather | solution.py:119
  1306.9 5.6 copy-start.12
  1413.5 35.3 %copy-start.6 = (f32[16,256,1,256]{1,3,2,0:T(8,128)S(1)}, f32[16,256,1,256]{1,3,2,0:T(8,128)}, u32[]{:S(2)}) copy-start(f32[16,256,1,256]{1,3,2,0:T(8,128)} %copy.111) | copy-start | bytes 12582916
  1448.8 4.8 copy-start.13
  1476.5 78.3 %copy-start.1 = (f32[1,1,8,256,256]{4,3,2,1,0:T(8,128)S(1)}, f32[1,1,8,256,256]{4,3,2,1,0:T(8,128)}, u32[]{:S(2)}) copy-start(f32[1,1,8,256,256]{4,3,2,1,0:T(8,128)} %param.10) | copy-start | bytes 6291460
Sparse Core Ops, SparseCore 0:
  1075.3 30.4 all-reduce.4
  1150.5 156.2 all-reduce.6
  1308.5 104.9 all-gather.1
